TPU v7x, 256 devices: a whole 4x4x8 slice. The times are simulated.
256 devices in a mesh: feature: 4 (over x), kvhead: 8 (over y, core), seq: 8 (over z).
Axes of the slice: x: 4, y: 4, z: 8, core: 2. Of those that a mesh axis runs over, the one named last changes fastest.
Arguments:
- queries: float32 [2048, 40, 128], P('seq', 'kvhead'), may hold values from -6 to 6
- keys: float32 [2048, 8, 128], P('seq', 'kvhead'), may hold values from -6 to 6
- values: float32 [2048, 8, 128], P('seq', 'kvhead'), may hold values from -6 to 6
- w_out: float32 [5120, 5120], P('kvhead', ('feature', 'seq')), may hold values from -0.078125 to 0.078125
Outputs:
- projected: float32 [2048, 5120], P(('seq', 'feature'), 'kvhead')
All inputs are finite; a program needn't handle non-finite values.
Results may differ from a plain program's by a relative error of at most 0.0003.
Values sent between devices are 32-bit elements; how exact they have to be, the bound alone decides.
A program may use at most 128 MiB of HBM per device.

v0:
```python
import math

import jax
import jax.numpy as jnp
import numpy as np
from jax import lax
from jax.sharding import PartitionSpec as P


def from_everyone(x, axis):
    copies = jnp.broadcast_to(x, (lax.axis_size(axis), *x.shape))
    return lax.all_to_all(copies, axis, split_axis=0, concat_axis=0, tiled=True)


def of_everyone(x, axis):
    everything = from_everyone(x, axis)
    return jnp.sum(everything, axis=0)


def in_blocks(x, dim, count):
    before, after = (x.shape[:dim], x.shape[dim + 1 :])
    return jnp.moveaxis(x.reshape(*before, count, -1, *after), dim, 0)


def summed_on_arrival(x, axis, dim):
    count = lax.axis_size(axis)
    blocks = lax.all_to_all(in_blocks(x, dim, count), axis, 0, 0, tiled=True)
    return jnp.sum(blocks, axis=0)


def expand(vectors, select_first, select_second, factor):
    highest = lax.Precision.HIGHEST
    left = jnp.einsum("...d,df->...f", vectors, select_first, precision=highest)
    right = jnp.einsum("...d,df->...f", vectors, select_second, precision=highest)
    return left * right * factor


def local(queries, keys, values, w_out):
    rows, local_heads, head_size = queries.shape
    kv_local = keys.shape[1]
    group = local_heads // kv_local
    parts = lax.axis_size("feature")
    position = lax.axis_index("feature")
    width = head_size * (head_size + 1) // 2 // parts
    upper_i, upper_j = np.triu_indices(head_size)
    factor_table = np.where(upper_i == upper_j, 1.0, math.sqrt(2.0)).astype(np.float32)
    first = lax.dynamic_slice_in_dim(jnp.asarray(upper_i.astype(np.int32)), position * width, width)
    second = lax.dynamic_slice_in_dim(
        jnp.asarray(upper_j.astype(np.int32)), position * width, width
    )
    factor = lax.dynamic_slice_in_dim(jnp.asarray(factor_table), position * width, width)
    entries = jnp.arange(head_size, dtype=jnp.int32)
    select_first = (entries[:, None] == first[None, :]).astype(jnp.float32)
    select_second = (entries[:, None] == second[None, :]).astype(jnp.float32)
    quarter = rows // parts
    scaled = (queries * head_size ** (-0.5)).reshape(rows, kv_local, group, head_size)
    highest = lax.Precision.HIGHEST
    block_states = []
    block_norms = []
    for block in range(parts):
        key_part = keys[block * quarter : (block + 1) * quarter]
        lifted = expand(key_part, select_first, select_second, factor)
        block_states.append(
            jnp.einsum(
                "tkf,tkd->kfd",
                lifted,
                values[block * quarter : (block + 1) * quarter],
                precision=highest,
            )
        )
        block_norms.append(jnp.sum(lifted, axis=0))
    total_state = sum(block_states)
    total_norm = sum(block_norms)
    own_index = lax.axis_index("seq")
    empty = (jnp.zeros_like(total_state), jnp.zeros_like(total_norm))
    pieces = (
        lax.all_gather(total_state[None], "seq", axis=0, tiled=True),
        lax.all_gather(total_norm[None], "seq", axis=0, tiled=True),
    )
    count = pieces[0].shape[0]
    keep = (jnp.arange(count, dtype=jnp.int32) < own_index).astype(jnp.float32)
    prior_state = empty[0] + jnp.einsum("n,nkfd->kfd", keep, pieces[0], precision=highest)
    prior_norm = empty[1] + jnp.einsum("n,nkf->kf", keep, pieces[1], precision=highest)
    running_state = prior_state
    running_norm = prior_norm
    numerators = []
    denominators = []
    for block in range(parts):
        lifted_query = expand(
            scaled[block * quarter : (block + 1) * quarter], select_first, select_second, factor
        )
        numerators.append(
            jnp.einsum("tkgf,kfd->tkgd", lifted_query, running_state, precision=highest)
        )
        denominators.append(
            jnp.einsum("tkgf,kf->tkg", lifted_query, running_norm, precision=highest)
        )
        running_state = running_state + block_states[block]
        running_norm = running_norm + block_norms[block]
    numerator = jnp.concatenate(numerators, axis=0)
    denominator = jnp.concatenate(denominators, axis=0)
    own_start = position * quarter
    own_query = lax.dynamic_slice_in_dim(scaled, own_start, quarter, 0)
    own_key = lax.dynamic_slice_in_dim(keys, own_start, quarter, 0)
    own_value = lax.dynamic_slice_in_dim(values, own_start, quarter, 0)
    scores = jnp.einsum("tkgd,skd->kgts", own_query, own_key, precision=highest)
    causal = jnp.tril(jnp.ones((quarter, quarter), jnp.bool_))
    squared = jnp.where(causal[None, None], scores * scores, jnp.float32(0.0))
    inner_numerator = jnp.einsum("kgts,skd->tkgd", squared, own_value, precision=highest)
    inner_denominator = jnp.transpose(jnp.sum(squared, axis=-1), (2, 0, 1))
    numerator = lax.dynamic_update_slice_in_dim(
        numerator,
        lax.dynamic_slice_in_dim(numerator, own_start, quarter, 0) + inner_numerator,
        own_start,
        0,
    )
    denominator = lax.dynamic_update_slice_in_dim(
        denominator,
        lax.dynamic_slice_in_dim(denominator, own_start, quarter, 0) + inner_denominator,
        own_start,
        0,
    )
    whole_numerator, whole_denominator = (
        of_everyone(numerator, "feature"),
        of_everyone(denominator, "feature"),
    )
    share_numerator = lax.dynamic_slice_in_dim(whole_numerator, own_start, quarter, 0)
    share_denominator = lax.dynamic_slice_in_dim(whole_denominator, own_start, quarter, 0)
    attended = (share_numerator / (share_denominator[..., None] + 1.0)).reshape(
        quarter, local_heads * head_size
    )
    partial_out = jnp.dot(
        attended,
        lax.all_gather(w_out, ("feature", "seq"), axis=1, tiled=True),
        precision=highest,
        preferred_element_type=jnp.float32,
    )
    return summed_on_arrival(partial_out, "kvhead", 1)


def solution(mesh):
    in_specs = (
        P("seq", "kvhead", None),
        P("seq", "kvhead", None),
        P("seq", "kvhead", None),
        P("kvhead", ("feature", "seq")),
    )
    out_specs = P(("seq", "feature"), "kvhead")
    return jax.shard_map(local, mesh=mesh, in_specs=in_specs, out_specs=out_specs, check_vma=False)
```

profile of v0, /device:TPU:1, one launch (start us, length us, event | category | flops | bytes accessed | tf_op | source)
XLA Modules:
  0.0 359.7 jit_solution(14535412155245520975)
XLA Ops:
  6.5 0.8 dynamic_slice.24
  7.3 0.8 dynamic_slice.26
  8.1 0.8 dynamic_slice.25
  8.9 0.8 constant_dynamic-slice_fusion.1
  9.8 0.9 fusion.26
  10.6 0.9 fusion.27
  11.5 0.9 fusion.82
  12.3 0.9 fusion.83
  13.2 0.9 fusion.25
  14.1 1.7 fusion.84
  15.7 0.9 fusion.28
  16.6 1.7 fusion.85
  18.2 0.6 dynamic-slice.12
  19.5 0.1 add_dynamic-update-slice_fusion
  19.7 0.6 copy-done.9
  20.3 0.0 all-reduce.3.cloned.1.call-update
  20.3 0.2 all-gather.7.cloned.1.call-start
  20.6 1.9 fusion.90
  22.4 1.9 fusion.89
  24.3 1.9 fusion.88
  26.2 2.9 convolution_add_fusion
  29.2 0.3 all-gather.5.cloned.1.call-start
  29.4 0.5 all-gather.5.cloned.1.call-update
  29.9 1.1 broadcast_multiply_fusion
  31.1 0.5 fusion.87
  31.6 1.4 fusion.29
  33.0 1.4 fusion.31
  34.4 1.4 fusion.33
  35.8 1.4 fusion.35
  37.1 3.1 fusion.2
  40.2 3.1 fusion.3
  43.4 3.1 fusion.4
  46.5 3.0 fusion.5
  49.5 40.5 %all-reduce.3.cloned.1.call-done = f32[16512]{0:T(1024)} async-done(((f32[16512]{0:T(1024)}), f32[16512]{0:T(1024)}) %all-reduce.3.cloned.1.call-update) | async-done | bytes 66064
  90.1 1.0 reshape.274
  91.0 0.2 fusion.86
  91.3 5.7 %convolution_bitcast_fusion.6 = f32[64,1,5]{0,1,2:T(1,128)S(1)} fusion(f32[2064,1,1]{0,1,2:T(1,128)S(1)} %reshape.303, f32[64,5,2064]{2,0,1:T(8,128)} %fusion.2), kind=kOutput, calls=%fused_computation.31 | convolution fusion | flops 7925760 | bytes 2651456 | tf_op jit(solution)/shard_map/tkgf,kf->tkg/dot_general | solution.py:96
  97.0 3.3 convolution_bitcast_fusion.7
  100.3 3.3 convolution_bitcast_fusion.8
  103.6 3.3 convolution_bitcast_fusion.9
  107.0 0.1 pad_maximum_fusion.1
  107.1 0.1 constant_dynamic-slice_fusion
  107.2 0.2 dynamic_update_slice.21
  107.4 0.6 broadcast_in_dim.20
  108.0 4.1 %all-to-all-start.1 = ((f32[4,256,1,5]{1,2,3,0:T(1,128)}), f32[4,256,1,5]{1,2,3,0:T(1,128)S(1)}, u32[]{:S(2)}, u32[]{:S(2)}) async-start(f32[4,256,1,5]{1,2,3,0:T(1,128)} %broadcast_in_dim.20), calls=%async_computation.1 | async-start | bytes 40960 | tf_op jit(solution)/shard_map/all_to_all | solution.py:12
  112.1 77.6 %all-gather.7.cloned.1.call-done = f32[16512,128]{1,0:T(8,128)} async-done(((f32[2064,128]{1,0:T(8,128)}), f32[16512,128]{1,0:T(8,128)}) %all-gather.7.cloned.1.call-update) | async-done | bytes 8454160 | tf_op jit(solution)/shard_map/all_gather | solution.py:77
  189.7 9.6 %fusion = f32[1,2064,128]{2,0,1:T(1,128)S(1)} fusion(f32[8,2064,128]{2,1,0:T(8,128)} %bitcast.154, s32[]{:T(128)S(6)} %axis_index.22), kind=kOutput, calls=%fused_computation | convolution fusion | flops 25362440 | bytes 9510916 | tf_op jit(solution)/shard_map/n,nkfd->kfd/dot_general | solution.py:82
  199.3 2.4 convolution_bitcast_fusion.5
  201.8 2.4 convolution_bitcast_fusion.4
  204.2 2.7 convolution_bitcast_fusion.3
  206.9 2.5 convolution_bitcast_fusion.2
  209.4 0.1 pad_maximum_fusion
  209.6 0.4 fusion.13
  210.0 1.7 broadcast_in_dim.19
  211.8 4.0 %all-to-all-start = ((f32[4,256,1,5,128]{4,1,3,2,0:T(8,128)}), f32[4,256,1,5,128]{4,1,3,2,0:T(8,128)S(1)}, u32[]{:S(2)}, u32[]{:S(2)}) async-start(f32[4,256,1,5,128]{4,1,3,2,0:T(8,128)} %broadcast_in_dim.19), calls=%async_computation | async-start | bytes 5242880 | tf_op jit(solution)/shard_map/all_to_all | solution.py:12
  215.8 0.1 dynamic-slice_add_fusion
  215.8 32.7 %all-to-all-done = f32[4,256,1,5,128]{4,1,3,2,0:T(8,128)S(1)} async-done(((f32[4,256,1,5,128]{4,1,3,2,0:T(8,128)}), f32[4,256,1,5,128]{4,1,3,2,0:T(8,128)S(1)}, u32[]{:S(2)}, u32[]{:S(2)}) %all-to-all-start) | async-done | bytes 2621472 | tf_op jit(solution)/shard_map/all_to_all | solution.py:12
  248.6 0.2 reduce_sum.74
  248.8 0.1 dynamic-slice_divide_fusion
  248.9 0.1 copy.16
  249.1 64.6 %all-gather.5.cloned.1.call-done = f32[640,5120]{0,1:T(8,128)} async-done(((f32[640,160]{0,1:T(8,128)}), f32[640,5120]{0,1:T(8,128)}) %all-gather.5.cloned.1.call-update) | async-done | bytes 13107216 | tf_op jit(solution)/shard_map/all_gather | solution.py:134
  313.6 15.7 %convolution_bitcast_fusion = f32[8,64,640]{2,1,0:T(8,128)S(1)} fusion(f32[64,640,1]{1,0,2:T(8,128)S(1)} %reshape.305, f32[8,640,640]{2,1,0:T(8,128)} %bitcast.153), kind=kOutput, calls=%fused_computation.19 | convolution fusion | flops 2516582400 | bytes 14581760 | tf_op jit(solution)/shard_map/dot_general | solution.py:132
  329.4 22.8 %all_to_all.15 = f32[8,64,640]{2,1,0:T(8,128)S(1)} all-to-all(f32[8,64,640]{2,1,0:T(8,128)S(1)} %convolution_bitcast_fusion), channel_id=1, replica_groups=mesh['feature'=4,'kvhead'=8,'seq'=8] {'kvhead'}, dimensions={0} | all-to-all | bytes 2621440 | tf_op jit(solution)/shard_map/all_to_all | solution.py:27
  352.2 0.7 reduce_sum.82
  (37 shorter events, 0.2 us)
Async XLA Ops:
  6.5 83.5 %all-reduce.3.cloned.1.call-start = ((), (), s32[]{:S(2)}) async-start(), calls=%async_computation.5 | async-start | bytes 139264
  15.7 2.5 copy-start.11
  15.7 4.8 %copy-start.10 = (f32[256,1,128]{2,1,0:T(1,128)S(1)}, f32[256,1,128]{2,1,0:T(1,128)}, u32[]{:S(2)}) copy-start(f32[256,1,128]{2,1,0:T(1,128)} %param.9) | copy-start | bytes 393220
  19.6 0.6 copy-start.9
  20.3 169.4 %all-gather.7.cloned.1.call-start = ((), (), s32[]{:S(2)}) async-start(), calls=%async_computation.4 | async-start | bytes 9510912 | tf_op jit(solution)/shard_map/all_gather | solution.py:77
  22.4 1.9 copy-start.8
  24.3 1.9 copy-start.7
  29.2 284.5 %all-gather.5.cloned.1.call-start = ((), (), s32[]{:S(2)}) async-start(), calls=%async_computation.3 | async-start | bytes 13516800 | tf_op jit(solution)/shard_map/all_gather | solution.py:134
  91.3 5.7 %copy-start.1 = (f32[64,5,2064]{2,0,1:T(8,128)S(1)}, f32[64,5,2064]{2,0,1:T(8,128)}, u32[]{:S(2)}) copy-start(f32[64,5,2064]{2,0,1:T(8,128)} %fusion.3) | copy-start | bytes 7925764
  96.9 3.3 copy-start.3
  100.3 3.3 copy-start.5
  108.0 102.0 %all-to-all-start.1 = ((f32[4,256,1,5]{1,2,3,0:T(1,128)}), f32[4,256,1,5]{1,2,3,0:T(1,128)S(1)}, u32[]{:S(2)}, u32[]{:S(2)}) async-start(f32[4,256,1,5]{1,2,3,0:T(1,128)} %broadcast_in_dim.20), calls=%async_computation.1 | async-start | bytes 40960 | tf_op jit(solution)/shard_map/all_to_all | solution.py:12
  189.7 9.6 %copy-start.6 = (f32[64,5,2064]{2,0,1:T(8,128)S(1)}, f32[64,5,2064]{2,0,1:T(8,128)}, u32[]{:S(2)}) copy-start(f32[64,5,2064]{2,0,1:T(8,128)} %fusion.5) | copy-start | bytes 7925764
  199.3 2.4 copy-start.4
  201.7 2.4 copy-start.2
  204.2 2.7 copy-start
  211.8 36.8 %all-to-all-start = ((f32[4,256,1,5,128]{4,1,3,2,0:T(8,128)}), f32[4,256,1,5,128]{4,1,3,2,0:T(8,128)S(1)}, u32[]{:S(2)}, u32[]{:S(2)}) async-start(f32[4,256,1,5,128]{4,1,3,2,0:T(8,128)} %broadcast_in_dim.19), calls=%async_computation | async-start | bytes 5242880 | tf_op jit(solution)/shard_map/all_to_all | solution.py:12
Sparse Core Ops, SparseCore 0:
  20.4 69.5 all-reduce.2
  91.8 97.8 all-gather.6
  192.3 121.2 all-gather.4
where the time goes:
time: 365 us; the launch traced here: 360 us
  waiting for transfers between devices  216 us (59%)
  matrix products  87.1 us (24%)
  blocking collectives  22.8 us (6%)
  between operations  14.4 us (4%)
  starting transfers between devices  8.51 us (2%)
  local copies, waits for them, and re-layouts  8.29 us (2%)
    all_gather x1, waiting for transfers between devices, local(): lax.all_gather(total_state[None], 'seq', axis=0, tiled=True)  77.6 us
    all_gather x1, waiting for transfers between devices, local(): lax.all_gather(w_out, ('feature', 'seq'), axis=1, tiled=True)  64.6 us
    unnamed x4, waiting for transfers between devices  41 us
    all_to_all x2, waiting for transfers between devices, from_everyone(): return lax.all_to_all(copies, axis, split_axis=0, concat_axis=0, tiled=True)  32.7 us
    all_to_all x1, blocking collectives, summed_on_arrival(): blocks = lax.all_to_all(in_blocks(x, dim, count), axis, 0, 0, tiled=True)  22.8 us
    dot_general x8, matrix products, expand(): jnp.einsum('...d,df->...f', vectors, select_second, precision=highest)  17.4 us
    dot_general x1, matrix products, local(): jnp.dot(attended, lax.all_gather(w_out, ('feature', 'seq'), axis=1, tiled...  15.7 us
    dot_general x4, matrix products, local(): jnp.einsum('tkgf,kf->tkg', lifted_query, running_norm, precision=highest)  15.7 us
  transfers between devices with their start and end apart: 5, of which 4 were waited for; matrix products, arithmetic and copies ran while one was open for 19% of the time, Pallas kernels for 0%

commit v1 on v0

v1 whole, which is shorter than its diff:
```python
import functools

import jax
import jax.numpy as jnp
from jax import lax
from jax.experimental import pallas as pl
from jax.experimental.pallas import tpu as pltpu
from jax.sharding import PartitionSpec as P

MESH = pl.DeviceIdType.MESH
NT = (((1,), (1,)), ((), ()))
F32 = jnp.float32
BF16 = jnp.bfloat16


def halves(x):
    high = x.astype(BF16)
    return high, (x - high.astype(F32)).astype(BF16)


def dot(a, b):
    return jnp.dot(a, b, preferred_element_type=F32)


def dot_nt(a, b):
    return lax.dot_general(a, b, NT, preferred_element_type=F32)


def kernel(
    q_hbm, k_hbm, v_hbm, w_hbm, o_ref,
    qv, kv, wt, qcat, kcat, klow, vcat, rs_src, rs_rcv, abuf, wh, wl, cpk, c1r, red, c2r,
    load_sem, kv_send, kv_recv, w_send, w_recv, rs_send, rs_recv, a_send, a_recv, c1_send, c1_recv, c2_send, c2_recv,
):
    group, rows, hd = q_hbm.shape
    parts = wt.shape[0]
    count = kv.shape[0]
    heads = c1r.shape[1]
    quarter = rows // parts
    half = count // 2
    wide = w_hbm.shape[0]
    rest = wide - hd
    lanes = hd // parts
    f = lax.axis_index("feature")
    k = lax.axis_index("kvhead")
    s = lax.axis_index("seq")
    y, c = lax.div(k, 2), lax.rem(k, 2)
    twin = k + 1 - 2 * c
    seq_half = lax.div(s, half)

    def at_z(d):
        return lax.rem(s + d + count, count)

    def at_x(d):
        return lax.rem(f + d + parts, parts)

    right, left = at_z(1), at_z(-1)

    own = pl.ds(pl.multiple_of(f * quarter, quarter), quarter)
    loads = [
        pltpu.make_async_copy(w_hbm, wt.at[f], load_sem.at[0]),
        pltpu.make_async_copy(k_hbm.at[own], kv.at[s, 0], load_sem.at[1]),
        pltpu.make_async_copy(v_hbm.at[own], kv.at[s, 1], load_sem.at[2]),
        pltpu.make_async_copy(q_hbm, qv, load_sem.at[3]),
    ]
    for load in loads:
        load.start()

    barrier = pltpu.get_barrier_semaphore()
    peers = 0
    for d in range(1, parts):
        pl.semaphore_signal(barrier, inc=1, device_id={"feature": at_x(d)}, device_id_type=MESH)
        peers += 1
    for d in range(1, count):
        pl.semaphore_signal(barrier, inc=1, device_id={"seq": at_z(d)}, device_id_type=MESH)
        pl.semaphore_signal(barrier, inc=1, device_id={"kvhead": twin, "seq": at_z(d)}, device_id_type=MESH)
        peers += 2
    for d in range(1, heads):
        pl.semaphore_signal(barrier, inc=1, device_id={"kvhead": lax.rem(k + d, heads)}, device_id_type=MESH)
        peers += 1
    for load in loads[:3]:
        load.wait()
    pl.semaphore_wait(barrier, peers)

    def remote(src, dst, send, recv, where):
        return pltpu.make_async_remote_copy(
            src_ref=src, dst_ref=dst, send_sem=send, recv_sem=recv, device_id=where, device_id_type=MESH
        )

    def kv_copy(i, slot, where):
        return remote(kv.at[slot], kv.at[slot], kv_send.at[i], kv_recv.at[i], {"seq": where})

    def kv_fwd(t):
        return kv_copy(t, at_z(-t), right)

    def kv_bwd(t):
        return kv_copy(half + t, at_z(t), left)

    def kv_take(slot):
        place = pl.ds(pl.multiple_of(slot * quarter, quarter), quarter)
        kh, kl = halves(kv[slot, 0])
        vh, vl = halves(kv[slot, 1])
        kcat[place, :hd] = kh
        kcat[place, hd:] = kh
        klow[place, :] = kl
        vcat[place, :hd] = vh
        vcat[place, hd:] = vl

    kv_fwd(0).start()
    kv_bwd(0).start()

    def w_copy(i, src, where):
        return remote(src, src, w_send.at[i], w_recv.at[i], {"feature": where})

    w_top, w_low = pl.ds(0, wide // 2), pl.ds(wide // 2, wide // 2)
    w_steps = [
        w_copy(0, wt.at[f], at_x(1)),
        w_copy(1, wt.at[f], at_x(-1)),
        w_copy(2, wt.at[at_x(-1), w_top], at_x(1)),
        w_copy(3, wt.at[at_x(1), w_low], at_x(-1)),
    ]
    w_takes = [
        w_copy(0, wt.at[at_x(-1)], at_x(1)),
        w_copy(1, wt.at[at_x(1)], at_x(-1)),
        w_copy(2, wt.at[at_x(2), w_top], at_x(1)),
        w_copy(3, wt.at[at_x(2), w_low], at_x(-1)),
    ]
    w_steps[0].start()
    w_steps[1].start()

    loads[3].wait()
    for g in range(group):
        qh, ql = halves(qv[g] * (hd ** -0.5))
        qcat[g, :, :hd] = qh
        qcat[g, :, hd:] = ql
    kv_take(s)
    for t in range(1, half + 1):
        kv_copy(t - 1, at_z(-t), right).wait_recv()
        if t < half:
            kv_fwd(t).start()
            kv_copy(half + t - 1, at_z(t), left).wait_recv()
            if t < half - 1:
                kv_bwd(t).start()
            kv_take(at_z(t))
        kv_take(at_z(-t))

    def rs_copy(d, g):
        to = at_x(d)
        return remote(rs_src.at[g, to], rs_rcv.at[d - 1, g], rs_send.at[d - 1, g], rs_recv.at[d - 1, g], {"feature": to})

    shape = (rows, count * quarter)
    column = lax.broadcasted_iota(jnp.int32, shape, 1)
    key_pos = lax.shift_right_logical(column, 6) * rows + f * quarter + jnp.bitwise_and(column, quarter - 1)
    query_pos = s * rows + lax.broadcasted_iota(jnp.int32, shape, 0)
    allowed = key_pos <= query_pos
    diagonal = lax.broadcasted_iota(jnp.int32, (quarter, hd), 0) == lax.broadcasted_iota(jnp.int32, (quarter, hd), 1)

    def head(g, carry):
        scores = dot_nt(qcat[g], kcat[...]) + dot_nt(qcat[g, :, :hd], klow[...])
        squared = jnp.where(allowed, scores * scores, 0.0)
        ph, plow = halves(squared)
        both = dot(ph, vcat[...])
        numerator = both[:, :hd] + both[:, hd:] + dot(plow, vcat[:, :hd])
        denominator = jnp.sum(squared, axis=1, keepdims=True)
        for p in range(parts):
            part = slice(p * quarter, (p + 1) * quarter)
            rs_src[g, p, :quarter] = numerator[part]
            spread = jnp.where(diagonal, jnp.broadcast_to(denominator[part], (quarter, hd)), 0.0)
            line = jnp.sum(spread, axis=0, keepdims=True)
            rs_src[g, p, quarter:] = jnp.broadcast_to(line, (8, hd))
        for d in range(1, parts):
            rs_copy(d, g).start()
        return carry

    lax.fori_loop(0, group, head, 0)

    w_takes[0].wait_recv()
    w_takes[1].wait_recv()
    w_steps[2].start()
    w_steps[3].start()

    def a_copy(i, g, slot, where):
        return remote(abuf.at[slot, g], abuf.at[slot, g], a_send.at[i, g], a_recv.at[i, g], {"seq": where})

    def normalize(g, carry):
        for d in range(1, parts):
            rs_copy(d, g).wait_recv()
        total = rs_src[g, f] + rs_rcv[0, g]
        for d in range(1, parts - 1):
            total = total + rs_rcv[d, g]
        line = jnp.broadcast_to(total[quarter:quarter + 1], (quarter, hd))
        denominator = jnp.sum(jnp.where(diagonal, line, 0.0), axis=1, keepdims=True)
        abuf[s, g] = total[:quarter] / (denominator + 1.0)
        a_copy(0, g, s, right).start()
        a_copy(half, g, s, left).start()
        return carry

    lax.fori_loop(0, group, normalize, 0)

    w_takes[2].wait_recv()
    w_takes[3].wait_recv()
    for p in range(parts):
        high, low = halves(wt[p])
        wh[p * hd:(p + 1) * hd] = high[:hd]
        wl[p * hd:(p + 1) * hd] = low[:hd]
        wh[parts * hd + p * rest:parts * hd + (p + 1) * rest] = high[hd:]
        wl[parts * hd + p * rest:parts * hd + (p + 1) * rest] = low[hd:]

    lane_group = lax.div(lax.broadcasted_iota(jnp.int32, (quarter // parts, hd), 1), rest)
    sub = quarter // parts

    def c1_copy(i, p, where, j):
        return remote(cpk.at[i, p], c1r.at[j, k], c1_send.at[i, p], c1_recv.at[j, k], {"kvhead": where})

    def c1_each(i, act):
        h, j = lax.div(i, half), lax.rem(i, half)
        for d in range(1, parts):
            p = lax.rem(y + d, parts)
            act(c1_copy(i, p, 2 * p + h, j))

        @pl.when(h != c)
        def _():
            act(c1_copy(i, y, twin, j))

    def project(slots):
        a = jnp.concatenate(
            [jnp.concatenate([abuf[i, g] for g in range(group)], axis=1) for i in slots], axis=0
        )
        n = len(slots) * quarter
        high, low = halves(a)
        both = dot_nt(jnp.concatenate([high, low], axis=0), wh[...])
        out = both[:n] + both[n:] + dot_nt(high, wl[...])
        for m, i in enumerate(slots):
            block = out[m * quarter:(m + 1) * quarter]
            tail = block[:, parts * hd:]
            for p in range(parts):
                cpk[i, p, :quarter] = block[:, p * hd:(p + 1) * hd]
                packed = jnp.zeros((sub, hd), F32)
                for g in range(parts):
                    piece = tail[g * sub:(g + 1) * sub]
                    shift = (rest * (g - p)) % hd
                    if shift:
                        piece = pltpu.roll(piece, shift, 1)
                    packed = jnp.where(lane_group == g, piece, packed)
                cpk[i, p, quarter:] = packed
            c1_each(i, lambda copy: copy.start())

    project([s])

    def step(t, carry):
        for g in range(group):
            a_copy(t - 1, g, at_z(-t), right).wait_recv()
            a_copy(t, g, at_z(-t), right).start()
            a_copy(half + t - 1, g, at_z(t), left).wait_recv()

            @pl.when(t < half - 1)
            def _():
                a_copy(half + t, g, at_z(t), left).start()

        project([at_z(-t), at_z(t)])
        return carry

    lax.fori_loop(1, half, step, 0)
    for g in range(group):
        a_copy(half - 1, g, at_z(-half), right).wait_recv()
    project([at_z(-half)])

    def c2_copy(j, to):
        slot = lax.rem(s, half)
        return remote(red.at[j], c2r.at[slot], c2_send.at[j], c2_recv.at[slot], {"kvhead": 2 * y + seq_half, "seq": to})

    def reduce(j, carry):
        i = half * c + j
        total = cpk[i, y]
        for d in range(1, heads):
            other = lax.rem(k + d, heads)
            remote(cpk.at[i, y], c1r.at[j, other], c1_send.at[i, y], c1_recv.at[j, other], {"kvhead": twin}).wait_recv()
            total = total + c1r[j, other]

        @pl.when(i == s)
        def _():
            c2r[j] = total

        @pl.when(i != s)
        def _():
            red[j] = total
            c2_copy(j, i).start()

        return carry

    lax.fori_loop(0, half, reduce, 0)

    def arrive(j, carry):
        @pl.when(half * c + j != s)
        def _():
            remote(red.at[j], c2r.at[j], c2_send.at[j], c2_recv.at[j], {"kvhead": twin}).wait_recv()

        return carry

    lax.fori_loop(0, half, arrive, 0)

    lane = lax.broadcasted_iota(jnp.int32, (quarter, hd), 1)
    for tile in range(parts + 1):
        value = None
        if tile < parts:
            value = c2r[tile, :quarter]
            if tile:
                value = pltpu.roll(value, rest * tile, 1)
        if tile > 0:
            j = tile - 1
            before = c2r[j, :quarter]
            if j:
                before = pltpu.roll(before, rest * j, 1)
            packed = c2r[j, quarter:]
            tail = jnp.concatenate(
                [pltpu.roll(packed, (rest * (j - g)) % hd, 1) if (j - g) % parts else packed for g in range(parts)], axis=0
            )
            value = tail if value is None else jnp.where(lane < rest * tile, tail, value)
            if j:
                value = jnp.where(lane < rest * j, before, value)
        o_ref[:, tile * hd:(tile + 1) * hd] = value

    for t in range(half):
        kv_fwd(t).wait_send()
        if t < half - 1:
            kv_bwd(t).wait_send()
    for copy in w_steps:
        copy.wait_send()

    def drain(g, carry):
        for d in range(1, parts):
            rs_copy(d, g).wait_send()
        for t in range(half):
            a_copy(t, g, at_z(-t), right).wait_send()
            if t < half - 1:
                a_copy(half + t, g, at_z(t), left).wait_send()
        return carry

    lax.fori_loop(0, group, drain, 0)

    def drain_c1(i, carry):
        c1_each(i, lambda copy: copy.wait_send())
        return carry

    lax.fori_loop(0, count, drain_c1, 0)

    def drain_c2(j, carry):
        @pl.when(half * c + j != s)
        def _():
            c2_copy(j, half * c + j).wait_send()

        return carry

    lax.fori_loop(0, half, drain_c2, 0)


def local(queries, keys, values, w_out, *, parts, count, heads):
    rows, group, hd = queries.shape
    quarter = rows // parts
    depth, wide = w_out.shape
    half = count // 2
    packed = quarter * wide // hd
    columns = parts * wide
    keys_all = count * quarter
    dma = pltpu.SemaphoreType.DMA
    any_space = pl.BlockSpec(memory_space=pl.ANY)
    return pl.pallas_call(
        kernel,
        out_shape=jax.ShapeDtypeStruct((quarter, half * wide), F32),
        in_specs=[any_space] * 4,
        out_specs=pl.BlockSpec(memory_space=pltpu.VMEM),
        scratch_shapes=[
            pltpu.VMEM((group, rows, hd), F32),
            pltpu.VMEM((count, 2, quarter, hd), F32),
            pltpu.VMEM((parts, wide, depth), F32),
            pltpu.VMEM((group, rows, 2 * hd), BF16),
            pltpu.VMEM((keys_all, 2 * hd), BF16),
            pltpu.VMEM((keys_all, hd), BF16),
            pltpu.VMEM((keys_all, 2 * hd), BF16),
            pltpu.VMEM((group, parts, quarter + 8, hd), F32),
            pltpu.VMEM((parts - 1, group, quarter + 8, hd), F32),
            pltpu.VMEM((count, group, quarter, hd), F32),
            pltpu.VMEM((columns, depth), BF16),
            pltpu.VMEM((columns, depth), BF16),
            pltpu.VMEM((count, parts, packed, hd), F32),
            pltpu.VMEM((half, heads, packed, hd), F32),
            pltpu.VMEM((half, packed, hd), F32),
            pltpu.VMEM((half, packed, hd), F32),
            dma((4,)),
            dma((count - 1,)),
            dma((count - 1,)),
            dma((4,)),
            dma((4,)),
            dma((parts - 1, group)),
            dma((parts - 1, group)),
            dma((count - 1, group)),
            dma((count - 1, group)),
            dma((count, parts)),
            dma((half, heads)),
            dma((half,)),
            dma((half,)),
        ],
        compiler_params=pltpu.CompilerParams(
            collective_id=0, has_side_effects=True, vmem_limit_bytes=60 * 1024 * 1024
        ),
        name="power_attention",
    )(
        jnp.transpose(queries, (1, 0, 2)),
        keys.reshape(rows, hd),
        values.reshape(rows, hd),
        w_out.T,
    )


def solution(mesh):
    body = functools.partial(
        local, parts=mesh.shape["feature"], count=mesh.shape["seq"], heads=mesh.shape["kvhead"]
    )
    in_specs = (
        P("seq", "kvhead", None),
        P("seq", "kvhead", None),
        P("seq", "kvhead", None),
        P("kvhead", ("feature", "seq")),
    )
    out_specs = P(("seq", "feature"), "kvhead")
    return jax.shard_map(body, mesh=mesh, in_specs=in_specs, out_specs=out_specs, check_vma=False)
```

time: 365 us -> 65.7 us (0.18); the launches traced: 360 us -> 65.6 us
  waiting for transfers between devices: 216 us -> 0 us
  matrix products: 87.1 us -> 0 us
  Pallas kernels: 0 us -> 64 us
  blocking collectives: 22.8 us -> 0 us
  between operations: 14.4 us -> 0.01 us
  starting transfers between devices: 8.51 us -> 0 us
  local copies, waits for them, and re-layouts: 8.29 us -> 1.59 us
    all_gather x2 -> x0, waiting for transfers between devices: 142 us -> none  [the longest x1 77.6 us: local(): lax.all_gather(total_state[None], 'seq', axis=0, tiled=True)]
    dot_general x33 -> x0, matrix products: 87.1 us -> none  [the longest x8 17.4 us: expand(): jnp.einsum('...d,df->...f', vectors, select_second, precision=highest)]
    pallas_call x0 -> x1, Pallas kernels: none -> 64 us  [local(): pl.pallas_call(kernel, out_shape=jax.ShapeDtypeStruct((quarter, half * wi...]
    unnamed x4 -> x0, waiting for transfers between devices: 41 us -> none
    all_to_all x2 -> x0, waiting for transfers between devices: 32.7 us -> none  [from_everyone(): return lax.all_to_all(copies, axis, split_axis=0, concat_axis=0, tiled=True)]
    all_to_all x1 -> x0, blocking collectives: 22.8 us -> none  [summed_on_arrival(): blocks = lax.all_to_all(in_blocks(x, dim, count), axis, 0, 0, tiled=True)]
    all_to_all x2 -> x0, starting transfers between devices: 8.03 us -> none  [from_everyone(): return lax.all_to_all(copies, axis, split_axis=0, concat_axis=0, tiled=True)]
  transfers between devices with their start and end apart: 5 -> 0, of which waited for: 4 -> 0; matrix products, arithmetic and copies ran while one was open for 19% -> 0% of each run, Pallas kernels for 0% -> 0%
where the time goes in v1:
time: 65.7 us; the launch traced here: 65.6 us
  Pallas kernels  64 us (97%)
  local copies, waits for them, and re-layouts  1.59 us (2%)
    pallas_call x1, Pallas kernels, local(): pl.pallas_call(kernel, out_shape=jax.ShapeDtypeStruct((quarter, half * wi...  64 us
    unnamed x1, local copies, waits for them, and re-layouts  1.59 us

profile of v1, /device:TPU:1, one launch (start us, length us, event | category | flops | bytes accessed | tf_op | source)
XLA Modules:
  0.0 65.6 jit_solution(9936845463008477295)
XLA Ops:
  0.0 64.0 %power_attention.1 = f32[64,640]{1,0:T(8,128)} custom-call(f32[5,256,128]{2,1,0:T(8,128)} %bitcast.4, f32[256,128]{1,0:T(8,128)} %bitcast.6, f32[256,128]{1,0:T(8,128)} %bitcast.7, f32[160,640]{1,0:T(8,128)} %bitcast.5), custom_call_target="tpu_custom_call" | custom-call | tf_op jit(solution)/shard_map/power_attention/pallas_call | solution.py:366
  64.0 1.6 %copy.6 = f32[64,640]{1,0:T(8,128)} copy(f32[64,640]{1,0:T(8,128)} %power_attention.1) | data formatting | bytes 327680

commit v2 on v1

--- a/solution.py
+++ b/solution.py
@@ -28,13 +28,14 @@
 
 def kernel(
     q_hbm, k_hbm, v_hbm, w_hbm, o_ref,
-    qv, kv, wt, qcat, kcat, klow, vcat, rs_src, rs_rcv, abuf, wh, wl, cpk, c1r, red, c2r,
-    load_sem, kv_send, kv_recv, w_send, w_recv, rs_send, rs_recv, a_send, a_recv, c1_send, c1_recv, c2_send, c2_recv,
+    qv, kv, wt, qcat, kcat, klow, vcat, rs_src, rs_rcv, abuf, wh, wl, cpk, c0r, c1r, red, c2r,
+    load_sem, kv_send, kv_recv, w_send, w_recv, rs_send, rs_recv, a_send, a_recv,
+    c0_send, c0_recv, c1_send, c1_recv, c2_send, c2_recv,
 ):
     group, rows, hd = q_hbm.shape
     parts = wt.shape[0]
     count = kv.shape[0]
-    heads = c1r.shape[1]
+    heads = 2 * parts
     quarter = rows // parts
     half = count // 2
     wide = w_hbm.shape[0]
@@ -77,8 +78,8 @@
     for d in range(1, heads):
         pl.semaphore_signal(barrier, inc=1, device_id={"kvhead": lax.rem(k + d, heads)}, device_id_type=MESH)
         peers += 1
-    for load in loads[:3]:
-        load.wait()
+    loads[1].wait()
+    loads[2].wait()
     pl.semaphore_wait(barrier, peers)
 
     def remote(src, dst, send, recv, where):
@@ -86,14 +87,25 @@
             src_ref=src, dst_ref=dst, send_sem=send, recv_sem=recv, device_id=where, device_id_type=MESH
         )
 
-    def kv_copy(i, slot, where):
-        return remote(kv.at[slot], kv.at[slot], kv_send.at[i], kv_recv.at[i], {"seq": where})
-
-    def kv_fwd(t):
-        return kv_copy(t, at_z(-t), right)
-
-    def kv_bwd(t):
-        return kv_copy(half + t, at_z(t), left)
+    pieces = 4
+    piece = 2 * quarter // pieces
+    hops = (2, -2, 1, -1, 3, -3, 4)
+
+    def kv_copy(i, n, slot, where):
+        ref = kv.at[slot, n * piece // quarter, pl.ds(n * piece % quarter, piece)]
+        return remote(ref, ref, kv_send.at[i, n], kv_recv.at[i, n], {"seq": where})
+
+    def kv_from(i, n):
+        return kv_copy(i, n, at_z(-hops[i]), right)
+
+    def kv_out(i, n):
+        if i < 4:
+            return kv_copy(i, n, s, at_z(hops[i]))
+        if i < 6:
+            step = 2 if i == 4 else -2
+            return kv_copy(i, n, at_z(-step), at_z(step // 2))
+        step = 2 if n < pieces // 2 else -2
+        return kv_copy(i, n, at_z(-step), at_z(step))
 
     def kv_take(slot):
         place = pl.ds(pl.multiple_of(slot * quarter, quarter), quarter)
@@ -105,8 +117,9 @@
         vcat[place, :hd] = vh
         vcat[place, hd:] = vl
 
-    kv_fwd(0).start()
-    kv_bwd(0).start()
+    for i in range(4):
+        for n in range(pieces):
+            kv_out(i, n).start()
 
     def w_copy(i, src, where):
         return remote(src, src, w_send.at[i], w_recv.at[i], {"feature": where})
@@ -124,6 +137,7 @@
         w_copy(2, wt.at[at_x(2), w_top], at_x(1)),
         w_copy(3, wt.at[at_x(2), w_low], at_x(-1)),
     ]
+    loads[0].wait()
     w_steps[0].start()
     w_steps[1].start()
 
@@ -133,15 +147,21 @@
         qcat[g, :, :hd] = qh
         qcat[g, :, hd:] = ql
     kv_take(s)
-    for t in range(1, half + 1):
-        kv_copy(t - 1, at_z(-t), right).wait_recv()
-        if t < half:
-            kv_fwd(t).start()
-            kv_copy(half + t - 1, at_z(t), left).wait_recv()
-            if t < half - 1:
-                kv_bwd(t).start()
-            kv_take(at_z(t))
-        kv_take(at_z(-t))
+    for n in range(pieces):
+        kv_from(0, n).wait_recv()
+        kv_out(4, n).start()
+        if n < pieces // 2:
+            kv_out(6, n).start()
+        kv_from(1, n).wait_recv()
+        kv_out(5, n).start()
+        if n >= pieces // 2:
+            kv_out(6, n).start()
+    kv_take(at_z(-2))
+    kv_take(at_z(2))
+    for i in range(2, len(hops)):
+        for n in range(pieces):
+            kv_from(i, n).wait_recv()
+        kv_take(at_z(-hops[i]))
 
     def rs_copy(d, g):
         to = at_x(d)
@@ -173,15 +193,10 @@
 
     lax.fori_loop(0, group, head, 0)
 
-    w_takes[0].wait_recv()
-    w_takes[1].wait_recv()
-    w_steps[2].start()
-    w_steps[3].start()
-
     def a_copy(i, g, slot, where):
         return remote(abuf.at[slot, g], abuf.at[slot, g], a_send.at[i, g], a_recv.at[i, g], {"seq": where})
 
-    def normalize(g, carry):
+    def normalize(g):
         for d in range(1, parts):
             rs_copy(d, g).wait_recv()
         total = rs_src[g, f] + rs_rcv[0, g]
@@ -192,34 +207,71 @@
         abuf[s, g] = total[:quarter] / (denominator + 1.0)
         a_copy(0, g, s, right).start()
         a_copy(half, g, s, left).start()
-        return carry
-
-    lax.fori_loop(0, group, normalize, 0)
-
-    w_takes[2].wait_recv()
-    w_takes[3].wait_recv()
-    for p in range(parts):
+
+    def relay(t, g):
+        a_copy(t - 1, g, at_z(-t), right).wait_recv()
+        if t < half:
+            a_copy(t, g, at_z(-t), right).start()
+            a_copy(half + t - 1, g, at_z(t), left).wait_recv()
+            if t < half - 1:
+                a_copy(half + t, g, at_z(t), left).start()
+
+    def split_weights(p):
         high, low = halves(wt[p])
-        wh[p * hd:(p + 1) * hd] = high[:hd]
-        wl[p * hd:(p + 1) * hd] = low[:hd]
-        wh[parts * hd + p * rest:parts * hd + (p + 1) * rest] = high[hd:]
-        wl[parts * hd + p * rest:parts * hd + (p + 1) * rest] = low[hd:]
+        main = pl.ds(pl.multiple_of(p * hd, hd), hd)
+        tail = pl.ds(pl.multiple_of(parts * hd + p * rest, rest), rest)
+        wh[main, :] = high[:hd]
+        wl[main, :] = low[:hd]
+        wh[tail, :] = high[hd:]
+        wl[tail, :] = low[hd:]
 
     lane_group = lax.div(lax.broadcasted_iota(jnp.int32, (quarter // parts, hd), 1), rest)
     sub = quarter // parts
 
-    def c1_copy(i, p, where, j):
-        return remote(cpk.at[i, p], c1r.at[j, k], c1_send.at[i, p], c1_recv.at[j, k], {"kvhead": where})
-
-    def c1_each(i, act):
-        h, j = lax.div(i, half), lax.rem(i, half)
-        for d in range(1, parts):
-            p = lax.rem(y + d, parts)
-            act(c1_copy(i, p, 2 * p + h, j))
-
-        @pl.when(h != c)
-        def _():
-            act(c1_copy(i, y, twin, j))
+    def c0_copy(i):
+        j = lax.rem(i, half)
+        return remote(cpk.at[i], c0r.at[j], c0_send.at[i], c0_recv.at[j], {"kvhead": twin})
+
+    def c1_copy(i, d):
+        p = lax.rem(y + d, parts)
+        j = lax.rem(i, half)
+        return remote(cpk.at[i, p], c1r.at[j, d - 1], c1_send.at[j, d - 1], c1_recv.at[j, d - 1], {"kvhead": 2 * p + c})
+
+    def c2_copy(i):
+        j, slot = lax.rem(i, half), lax.rem(s, half)
+        return remote(red.at[j], c2r.at[slot], c2_send.at[j], c2_recv.at[slot], {"kvhead": 2 * y + seq_half, "seq": i})
+
+    def mine(i):
+        return lax.div(i, half) == c
+
+    def merge(slots):
+        for i in slots:
+            @pl.when(mine(i))
+            def _():
+                c0_copy(i).wait_recv()
+                for p in range(parts):
+                    cpk[i, p] = cpk[i, p] + c0r[lax.rem(i, half), p]
+                for d in range(1, parts):
+                    c1_copy(i, d).start()
+
+    def finish(slots):
+        for i in slots:
+            @pl.when(mine(i))
+            def _():
+                j = lax.rem(i, half)
+                total = cpk[i, y]
+                for d in range(1, parts):
+                    c1_copy(i, d).wait_recv()
+                    total = total + c1r[j, d - 1]
+
+                @pl.when(i == s)
+                def _():
+                    c2r[j] = total
+
+                @pl.when(i != s)
+                def _():
+                    red[j] = total
+                    c2_copy(i).start()
 
     def project(slots):
         a = jnp.concatenate(
@@ -242,52 +294,60 @@
                         piece = pltpu.roll(piece, shift, 1)
                     packed = jnp.where(lane_group == g, piece, packed)
                 cpk[i, p, quarter:] = packed
-            c1_each(i, lambda copy: copy.start())
-
-    project([s])
-
-    def step(t, carry):
-        for g in range(group):
-            a_copy(t - 1, g, at_z(-t), right).wait_recv()
-            a_copy(t, g, at_z(-t), right).start()
-            a_copy(half + t - 1, g, at_z(t), left).wait_recv()
-
-            @pl.when(t < half - 1)
+
+            @pl.when(jnp.logical_not(mine(i)))
             def _():
-                a_copy(half + t, g, at_z(t), left).start()
-
-        project([at_z(-t), at_z(t)])
-        return carry
-
-    lax.fori_loop(1, half, step, 0)
-    for g in range(group):
-        a_copy(half - 1, g, at_z(-half), right).wait_recv()
-    project([at_z(-half)])
-
-    def c2_copy(j, to):
-        slot = lax.rem(s, half)
-        return remote(red.at[j], c2r.at[slot], c2_send.at[j], c2_recv.at[slot], {"kvhead": 2 * y + seq_half, "seq": to})
-
-    def reduce(j, carry):
-        i = half * c + j
-        total = cpk[i, y]
-        for d in range(1, heads):
-            other = lax.rem(k + d, heads)
-            remote(cpk.at[i, y], c1r.at[j, other], c1_send.at[i, y], c1_recv.at[j, other], {"kvhead": twin}).wait_recv()
-            total = total + c1r[j, other]
-
-        @pl.when(i == s)
-        def _():
-            c2r[j] = total
-
-        @pl.when(i != s)
-        def _():
-            red[j] = total
-            c2_copy(j, i).start()
-
-        return carry
-
-    lax.fori_loop(0, half, reduce, 0)
+                c0_copy(i).start()
+
+
+    steps = [[s]] + [[at_z(-t), at_z(t)] for t in range(1, half)] + [[at_z(-half)]]
+    w_takes[0].wait_recv()
+    w_takes[1].wait_recv()
+    w_steps[2].start()
+    w_steps[3].start()
+    normalize(0)
+    for p in (0, -1, 1):
+        split_weights(at_x(p))
+    normalize(1)
+    relay(1, 0)
+    normalize(2)
+    relay(1, 1)
+    normalize(3)
+    relay(1, 2)
+    relay(2, 0)
+    normalize(4)
+    relay(1, 3)
+    relay(2, 1)
+    w_takes[2].wait_recv()
+    w_takes[3].wait_recv()
+    split_weights(at_x(2))
+    project(steps[0])
+    relay(1, 4)
+    relay(2, 2)
+    relay(3, 0)
+    relay(2, 3)
+    relay(3, 1)
+    project(steps[1])
+    relay(2, 4)
+    relay(3, 2)
+    relay(3, 3)
+    project(steps[2])
+    relay(3, 4)
+    for g in range(group - 1):
+        relay(half, g)
+    project(steps[3])
+    merge(steps[0])
+    merge(steps[1])
+    relay(half, group - 1)
+    project(steps[4])
+    merge(steps[2])
+    merge(steps[3])
+    merge(steps[4])
+    finish(steps[0])
+    finish(steps[1])
+    finish(steps[2])
+    finish(steps[3])
+    finish(steps[4])
 
     def arrive(j, carry):
         @pl.when(half * c + j != s)
@@ -319,10 +379,9 @@
                 value = jnp.where(lane < rest * j, before, value)
         o_ref[:, tile * hd:(tile + 1) * hd] = value
 
-    for t in range(half):
-        kv_fwd(t).wait_send()
-        if t < half - 1:
-            kv_bwd(t).wait_send()
+    for i in range(len(hops)):
+        for n in range(pieces):
+            kv_out(i, n).wait_send()
     for copy in w_steps:
         copy.wait_send()
 
@@ -337,23 +396,26 @@
 
     lax.fori_loop(0, group, drain, 0)
 
-    def drain_c1(i, carry):
-        c1_each(i, lambda copy: copy.wait_send())
+    def drain_c(i, carry):
+        @pl.when(mine(i))
+        def _():
+            for d in range(1, parts):
+                c1_copy(i, d).wait_send()
+
+            @pl.when(i != s)
+            def _():
+                c2_copy(i).wait_send()
+
+        @pl.when(jnp.logical_not(mine(i)))
+        def _():
+            c0_copy(i).wait_send()
+
         return carry
 
-    lax.fori_loop(0, count, drain_c1, 0)
-
-    def drain_c2(j, carry):
-        @pl.when(half * c + j != s)
-        def _():
-            c2_copy(j, half * c + j).wait_send()
-
-        return carry
-
-    lax.fori_loop(0, half, drain_c2, 0)
-
-
-def local(queries, keys, values, w_out, *, parts, count, heads):
+    lax.fori_loop(0, count, drain_c, 0)
+
+
+def local(queries, keys, values, w_out, *, parts, count):
     rows, group, hd = queries.shape
     quarter = rows // parts
     depth, wide = w_out.shape
@@ -365,7 +427,7 @@
     any_space = pl.BlockSpec(memory_space=pl.ANY)
     return pl.pallas_call(
         kernel,
-        out_shape=jax.ShapeDtypeStruct((quarter, half * wide), F32),
+        out_shape=pltpu.VMEM((quarter, half * wide), F32),
         in_specs=[any_space] * 4,
         out_specs=pl.BlockSpec(memory_space=pltpu.VMEM),
         scratch_shapes=[
@@ -382,20 +444,23 @@
             pltpu.VMEM((columns, depth), BF16),
             pltpu.VMEM((columns, depth), BF16),
             pltpu.VMEM((count, parts, packed, hd), F32),
-            pltpu.VMEM((half, heads, packed, hd), F32),
+            pltpu.VMEM((half, parts, packed, hd), F32),
+            pltpu.VMEM((half, parts - 1, packed, hd), F32),
             pltpu.VMEM((half, packed, hd), F32),
             pltpu.VMEM((half, packed, hd), F32),
             dma((4,)),
-            dma((count - 1,)),
-            dma((count - 1,)),
+            dma((count - 1, 4)),
+            dma((count - 1, 4)),
             dma((4,)),
             dma((4,)),
             dma((parts - 1, group)),
             dma((parts - 1, group)),
             dma((count - 1, group)),
             dma((count - 1, group)),
-            dma((count, parts)),
-            dma((half, heads)),
+            dma((count,)),
+            dma((half,)),
+            dma((half, parts - 1)),
+            dma((half, parts - 1)),
             dma((half,)),
             dma((half,)),
         ],
@@ -413,7 +478,7 @@
 
 def solution(mesh):
     body = functools.partial(
-        local, parts=mesh.shape["feature"], count=mesh.shape["seq"], heads=mesh.shape["kvhead"]
+        local, parts=mesh.shape["feature"], count=mesh.shape["seq"]
     )
     in_specs = (
         P("seq", "kvhead", None),

time: 65.7 us -> 63.6 us (0.968)
  Pallas kernels: 64 us -> 62.8 us
  local copies, waits for them, and re-layouts: 1.59 us -> 0.67 us
    pallas_call x1, Pallas kernels: 64 us -> 62.8 us  [local(): pl.pallas_call(kernel, out_shape=pltpu.VMEM((quarter, half * wide), F32),...]
    unnamed x1, local copies, waits for them, and re-layouts: 1.59 us -> 0.67 us
where the time goes in v2:
time: 63.6 us; the launch traced here: 63.5 us
  Pallas kernels  62.8 us (99%)
  local copies, waits for them, and re-layouts  0.67 us (1%)
    pallas_call x1, Pallas kernels, local(): pl.pallas_call(kernel, out_shape=pltpu.VMEM((quarter, half * wide), F32),...  62.8 us

profile of v2, /device:TPU:1, one launch (start us, length us, event | category | flops | bytes accessed | tf_op | source)
XLA Modules:
  0.0 63.5 jit_solution(7955090505639878049)
XLA Ops:
  0.0 62.8 %power_attention.1 = f32[64,640]{1,0:T(8,128)S(1)} custom-call(f32[5,256,128]{2,1,0:T(8,128)} %bitcast.4, f32[256,128]{1,0:T(8,128)} %bitcast.6, f32[256,128]{1,0:T(8,128)} %bitcast.7, f32[160,640]{1,0:T(8,128)} %bitcast.5), custom_call_target="tpu_custom_call" | custom-call | tf_op jit(solution)/shard_map/power_attention/pallas_call | solution.py:428
  62.8 0.7 %copy.6 = f32[64,640]{1,0:T(8,128)} copy(f32[64,640]{1,0:T(8,128)S(1)} %power_attention.1) | data formatting | bytes 327680

commit v3 on v2

--- a/solution.py
+++ b/solution.py
@@ -28,8 +28,8 @@
 
 def kernel(
     q_hbm, k_hbm, v_hbm, w_hbm, o_ref,
-    qv, kv, wt, qcat, kcat, klow, vcat, rs_src, rs_rcv, abuf, wh, wl, cpk, c0r, c1r, red, c2r,
-    load_sem, kv_send, kv_recv, w_send, w_recv, rs_send, rs_recv, a_send, a_recv,
+    qv, kv, wt, qcat, kcat, klow, vcat, rs_src, rs_rcv, den_src, den_rcv, abuf, wh, wl, cpk, c0r, c1r, red, c2r,
+    load_sem, kv_send, kv_recv, w_send, w_recv, rs_send, rs_recv, den_send, den_recv, a_send, a_recv,
     c0_send, c0_recv, c1_send, c1_recv, c2_send, c2_recv,
 ):
     group, rows, hd = q_hbm.shape
@@ -167,6 +167,12 @@
         to = at_x(d)
         return remote(rs_src.at[g, to], rs_rcv.at[d - 1, g], rs_send.at[d - 1, g], rs_recv.at[d - 1, g], {"feature": to})
 
+    def den_copy(d, g):
+        to = at_x(d)
+        return remote(
+            den_src.at[g, to], den_rcv.at[d - 1, g], den_send.at[d - 1, g], den_recv.at[d - 1, g], {"feature": to}
+        )
+
     shape = (rows, count * quarter)
     column = lax.broadcasted_iota(jnp.int32, shape, 1)
     key_pos = lax.shift_right_logical(column, 6) * rows + f * quarter + jnp.bitwise_and(column, quarter - 1)
@@ -183,11 +189,11 @@
         denominator = jnp.sum(squared, axis=1, keepdims=True)
         for p in range(parts):
             part = slice(p * quarter, (p + 1) * quarter)
-            rs_src[g, p, :quarter] = numerator[part]
+            rs_src[g, p] = numerator[part]
             spread = jnp.where(diagonal, jnp.broadcast_to(denominator[part], (quarter, hd)), 0.0)
-            line = jnp.sum(spread, axis=0, keepdims=True)
-            rs_src[g, p, quarter:] = jnp.broadcast_to(line, (8, hd))
+            den_src[g, p] = jnp.sum(spread, axis=0, keepdims=True)
         for d in range(1, parts):
+            den_copy(d, g).start()
             rs_copy(d, g).start()
         return carry
 
@@ -196,25 +202,70 @@
     def a_copy(i, g, slot, where):
         return remote(abuf.at[slot, g], abuf.at[slot, g], a_send.at[i, g], a_recv.at[i, g], {"seq": where})
 
+    ringed = 2
+
     def normalize(g):
         for d in range(1, parts):
+            den_copy(d, g).wait_recv()
             rs_copy(d, g).wait_recv()
         total = rs_src[g, f] + rs_rcv[0, g]
+        line = den_src[g, f] + den_rcv[0, g]
         for d in range(1, parts - 1):
             total = total + rs_rcv[d, g]
-        line = jnp.broadcast_to(total[quarter:quarter + 1], (quarter, hd))
+            line = line + den_rcv[d, g]
+        line = jnp.broadcast_to(line, (quarter, hd))
         denominator = jnp.sum(jnp.where(diagonal, line, 0.0), axis=1, keepdims=True)
-        abuf[s, g] = total[:quarter] / (denominator + 1.0)
-        a_copy(0, g, s, right).start()
-        a_copy(half, g, s, left).start()
+        abuf[s, g] = total / (denominator + 1.0)
+        if g < ringed:
+            a_copy(0, g, s, right).start()
+            a_copy(half, g, s, left).start()
+        else:
+            for i in range(4):
+                a_out(i, g).start()
+
+    def a_last(g):
+        if g % 2 == 0:
+            return a_copy(half - 1, g, at_z(1 - half), right)
+        return a_copy(half - 1, g, at_z(half - 1), left)
 
     def relay(t, g):
         a_copy(t - 1, g, at_z(-t), right).wait_recv()
         if t < half:
+            a_copy(half + t - 1, g, at_z(t), left).wait_recv()
+        if t < half - 1:
             a_copy(t, g, at_z(-t), right).start()
-            a_copy(half + t - 1, g, at_z(t), left).wait_recv()
-            if t < half - 1:
-                a_copy(half + t, g, at_z(t), left).start()
+            a_copy(half + t, g, at_z(t), left).start()
+        if t == half - 1:
+            a_last(g).start()
+
+    def a_from(i, g):
+        return a_copy(i, g, at_z(-hops[i]), right)
+
+    def a_out(i, g):
+        if i < 4:
+            return a_copy(i, g, s, at_z(hops[i]))
+        if i < 6:
+            step = 2 if i == 4 else -2
+            return a_copy(i, g, at_z(-step), at_z(step // 2))
+        step = 2 if g % 2 == 0 else -2
+        return a_copy(i, g, at_z(-step), at_z(step))
+
+    def forward(g):
+        a_from(0, g).wait_recv()
+        if g % 2 == 0:
+            a_out(6, g).start()
+        a_out(4, g).start()
+        a_from(1, g).wait_recv()
+        if g % 2 == 1:
+            a_out(6, g).start()
+        a_out(5, g).start()
+
+    def arrived(*distances):
+        for g in range(ringed, group):
+            for distance in distances:
+                for i, hop in enumerate(hops):
+                    if abs(hop) == distance:
+                        a_from(i, g).wait_recv()
 
     def split_weights(p):
         high, low = halves(wt[p])
@@ -300,59 +351,89 @@
                 c0_copy(i).start()
 
 
-    steps = [[s]] + [[at_z(-t), at_z(t)] for t in range(1, half)] + [[at_z(-half)]]
+    steps = [[s]] + [[at_z(-1), at_z(1)], [at_z(-2), at_z(2)], [at_z(-3), at_z(3), at_z(4)]]
+    normalize(0)
+    normalize(1)
+    normalize(2)
+    relay(1, 0)
+    normalize(3)
+    relay(1, 1)
+    normalize(4)
     w_takes[0].wait_recv()
     w_takes[1].wait_recv()
     w_steps[2].start()
     w_steps[3].start()
-    normalize(0)
     for p in (0, -1, 1):
         split_weights(at_x(p))
-    normalize(1)
-    relay(1, 0)
-    normalize(2)
-    relay(1, 1)
-    normalize(3)
-    relay(1, 2)
     relay(2, 0)
-    normalize(4)
-    relay(1, 3)
+    forward(2)
     relay(2, 1)
+    forward(3)
+    forward(4)
     w_takes[2].wait_recv()
     w_takes[3].wait_recv()
     split_weights(at_x(2))
     project(steps[0])
-    relay(1, 4)
-    relay(2, 2)
     relay(3, 0)
-    relay(2, 3)
+    arrived(1)
+    project(steps[1])
     relay(3, 1)
-    project(steps[1])
-    relay(2, 4)
-    relay(3, 2)
-    relay(3, 3)
+    merge(steps[0])
     project(steps[2])
-    relay(3, 4)
-    for g in range(group - 1):
-        relay(half, g)
+    merge(steps[1])
+    merge(steps[2])
+    relay(4, 0)
+    relay(4, 1)
+    arrived(3, 4)
     project(steps[3])
-    merge(steps[0])
-    merge(steps[1])
-    relay(half, group - 1)
-    project(steps[4])
-    merge(steps[2])
     merge(steps[3])
-    merge(steps[4])
     finish(steps[0])
     finish(steps[1])
     finish(steps[2])
     finish(steps[3])
-    finish(steps[4])
+
+    for i in range(len(hops)):
+        for n in range(pieces):
+            kv_out(i, n).wait_send()
+    for copy in w_steps:
+        copy.wait_send()
+
+    def drain(g, carry):
+        for d in range(1, parts):
+            rs_copy(d, g).wait_send()
+            den_copy(d, g).wait_send()
+        return carry
+
+    lax.fori_loop(0, group, drain, 0)
+    for g in range(group):
+        if g < ringed:
+            for t in range(half - 1):
+                a_copy(t, g, at_z(-t), right).wait_send()
+                a_copy(half + t, g, at_z(t), left).wait_send()
+            a_last(g).wait_send()
+        else:
+            for i in range(len(hops)):
+                a_out(i, g).wait_send()
+
+    def drain_c(i, carry):
+        @pl.when(mine(i))
+        def _():
+            for d in range(1, parts):
+                c1_copy(i, d).wait_send()
+
+        @pl.when(jnp.logical_not(mine(i)))
+        def _():
+            c0_copy(i).wait_send()
+
+        return carry
+
+    lax.fori_loop(0, count, drain_c, 0)
 
     def arrive(j, carry):
         @pl.when(half * c + j != s)
         def _():
             remote(red.at[j], c2r.at[j], c2_send.at[j], c2_recv.at[j], {"kvhead": twin}).wait_recv()
+            c2_copy(half * c + j).wait_send()
 
         return carry
 
@@ -378,41 +459,6 @@
             if j:
                 value = jnp.where(lane < rest * j, before, value)
         o_ref[:, tile * hd:(tile + 1) * hd] = value
-
-    for i in range(len(hops)):
-        for n in range(pieces):
-            kv_out(i, n).wait_send()
-    for copy in w_steps:
-        copy.wait_send()
-
-    def drain(g, carry):
-        for d in range(1, parts):
-            rs_copy(d, g).wait_send()
-        for t in range(half):
-            a_copy(t, g, at_z(-t), right).wait_send()
-            if t < half - 1:
-                a_copy(half + t, g, at_z(t), left).wait_send()
-        return carry
-
-    lax.fori_loop(0, group, drain, 0)
-
-    def drain_c(i, carry):
-        @pl.when(mine(i))
-        def _():
-            for d in range(1, parts):
-                c1_copy(i, d).wait_send()
-
-            @pl.when(i != s)
-            def _():
-                c2_copy(i).wait_send()
-
-        @pl.when(jnp.logical_not(mine(i)))
-        def _():
-            c0_copy(i).wait_send()
-
-        return carry
-
-    lax.fori_loop(0, count, drain_c, 0)
 
 
 def local(queries, keys, values, w_out, *, parts, count):
@@ -438,8 +484,10 @@
             pltpu.VMEM((keys_all, 2 * hd), BF16),
             pltpu.VMEM((keys_all, hd), BF16),
             pltpu.VMEM((keys_all, 2 * hd), BF16),
-            pltpu.VMEM((group, parts, quarter + 8, hd), F32),
-            pltpu.VMEM((parts - 1, group, quarter + 8, hd), F32),
+            pltpu.VMEM((group, parts, quarter, hd), F32),
+            pltpu.VMEM((parts - 1, group, quarter, hd), F32),
+            pltpu.VMEM((group, parts, 1, hd), F32),
+            pltpu.VMEM((parts - 1, group, 1, hd), F32),
             pltpu.VMEM((count, group, quarter, hd), F32),
             pltpu.VMEM((columns, depth), BF16),
             pltpu.VMEM((columns, depth), BF16),
@@ -453,6 +501,8 @@
             dma((count - 1, 4)),
             dma((4,)),
             dma((4,)),
+            dma((parts - 1, group)),
+            dma((parts - 1, group)),
             dma((parts - 1, group)),
             dma((parts - 1, group)),
             dma((count - 1, group)),

time: 63.6 us -> 60.4 us (0.950)
  Pallas kernels: 62.8 us -> 59.6 us
    pallas_call x1, Pallas kernels: 62.8 us -> 59.6 us  [local(): pl.pallas_call(kernel, out_shape=pltpu.VMEM((quarter, half * wide), F32),...]
where the time goes in v3:
time: 60.4 us; the launch traced here: 60.3 us
  Pallas kernels  59.6 us (99%)
  local copies, waits for them, and re-layouts  0.67 us (1%)
    pallas_call x1, Pallas kernels, local(): pl.pallas_call(kernel, out_shape=pltpu.VMEM((quarter, half * wide), F32),...  59.6 us

profile of v3, /device:TPU:1, one launch (start us, length us, event | category | flops | bytes accessed | tf_op | source)
XLA Modules:
  0.0 60.3 jit_solution(12712837192038340407)
XLA Ops:
  0.0 59.6 %power_attention.1 = f32[64,640]{1,0:T(8,128)S(1)} custom-call(f32[5,256,128]{2,1,0:T(8,128)} %bitcast.4, f32[256,128]{1,0:T(8,128)} %bitcast.6, f32[256,128]{1,0:T(8,128)} %bitcast.7, f32[160,640]{1,0:T(8,128)} %bitcast.5), custom_call_target="tpu_custom_call" | custom-call | tf_op jit(solution)/shard_map/power_attention/pallas_call | solution.py:474
  59.6 0.7 %copy.6 = f32[64,640]{1,0:T(8,128)} copy(f32[64,640]{1,0:T(8,128)S(1)} %power_attention.1) | data formatting | bytes 327680

commit v4 on v3

--- a/solution.py
+++ b/solution.py
@@ -31,6 +31,7 @@
     qv, kv, wt, qcat, kcat, klow, vcat, rs_src, rs_rcv, den_src, den_rcv, abuf, wh, wl, cpk, c0r, c1r, red, c2r,
     load_sem, kv_send, kv_recv, w_send, w_recv, rs_send, rs_recv, den_send, den_recv, a_send, a_recv,
     c0_send, c0_recv, c1_send, c1_recv, c2_send, c2_recv,
+    line_known, side_known, cross_known,
 ):
     group, rows, hd = q_hbm.shape
     parts = wt.shape[0]
@@ -67,20 +68,28 @@
         load.start()
 
     barrier = pltpu.get_barrier_semaphore()
-    peers = 0
-    for d in range(1, parts):
-        pl.semaphore_signal(barrier, inc=1, device_id={"feature": at_x(d)}, device_id_type=MESH)
-        peers += 1
-    for d in range(1, count):
-        pl.semaphore_signal(barrier, inc=1, device_id={"seq": at_z(d)}, device_id_type=MESH)
-        pl.semaphore_signal(barrier, inc=1, device_id={"kvhead": twin, "seq": at_z(d)}, device_id_type=MESH)
-        peers += 2
-    for d in range(1, heads):
-        pl.semaphore_signal(barrier, inc=1, device_id={"kvhead": lax.rem(k + d, heads)}, device_id_type=MESH)
-        peers += 1
+
+    def signal(semaphore, where):
+        pl.semaphore_signal(semaphore, inc=1, device_id=where, device_id_type=MESH)
+
+    beside = [{"kvhead": lax.rem(k + d, heads)} for d in (2, heads - 2)]
+    second = [{"seq": at_z(d)} for d in (2, -2)]
+    near = [{"feature": at_x(d)} for d in range(1, parts)] + [{"seq": right}, {"seq": left}, {"kvhead": twin}]
+    near = near + beside + second
+    for where in near:
+        signal(barrier, where)
     loads[1].wait()
     loads[2].wait()
-    pl.semaphore_wait(barrier, peers)
+    pl.semaphore_wait(barrier, len(near))
+    for where in second:
+        signal(line_known, where)
+    for where in beside:
+        signal(side_known, where)
+
+    def known():
+        pl.semaphore_wait(line_known, len(second))
+        pl.semaphore_wait(side_known, len(beside))
+        signal(cross_known, {"kvhead": twin})
 
     def remote(src, dst, send, recv, where):
         return pltpu.make_async_remote_copy(
@@ -369,6 +378,7 @@
     forward(2)
     relay(2, 1)
     forward(3)
+    known()
     forward(4)
     w_takes[2].wait_recv()
     w_takes[3].wait_recv()
@@ -387,6 +397,7 @@
     arrived(3, 4)
     project(steps[3])
     merge(steps[3])
+    pl.semaphore_wait(cross_known, 1)
     finish(steps[0])
     finish(steps[1])
     finish(steps[2])
@@ -513,6 +524,9 @@
             dma((half, parts - 1)),
             dma((half,)),
             dma((half,)),
+            pltpu.SemaphoreType.REGULAR,
+            pltpu.SemaphoreType.REGULAR,
+            pltpu.SemaphoreType.REGULAR,
         ],
         compiler_params=pltpu.CompilerParams(
             collective_id=0, has_side_effects=True, vmem_limit_bytes=60 * 1024 * 1024

time: 60.4 us -> 58.5 us (0.969)
  Pallas kernels: 59.6 us -> 57.8 us
    pallas_call x1, Pallas kernels: 59.6 us -> 57.8 us  [local(): pl.pallas_call(kernel, out_shape=pltpu.VMEM((quarter, half * wide), F32),...]
where the time goes in v4:
time: 58.5 us; the launch traced here: 58.4 us
  Pallas kernels  57.8 us (99%)
  local copies, waits for them, and re-layouts  0.67 us (1%)
    pallas_call x1, Pallas kernels, local(): pl.pallas_call(kernel, out_shape=pltpu.VMEM((quarter, half * wide), F32),...  57.8 us

profile of v4, /device:TPU:1, one launch (start us, length us, event | category | flops | bytes accessed | tf_op | source)
XLA Modules:
  0.0 58.4 jit_solution(14425334799282429493)
XLA Ops:
  0.0 57.8 %power_attention.1 = f32[64,640]{1,0:T(8,128)S(1)} custom-call(f32[5,256,128]{2,1,0:T(8,128)} %bitcast.4, f32[256,128]{1,0:T(8,128)} %bitcast.6, f32[256,128]{1,0:T(8,128)} %bitcast.7, f32[160,640]{1,0:T(8,128)} %bitcast.5), custom_call_target="tpu_custom_call" | custom-call | tf_op jit(solution)/shard_map/power_attention/pallas_call | solution.py:485
  57.8 0.7 %copy.6 = f32[64,640]{1,0:T(8,128)} copy(f32[64,640]{1,0:T(8,128)S(1)} %power_attention.1) | data formatting | bytes 327680

commit v5 on v4

--- a/solution.py
+++ b/solution.py
@@ -147,30 +147,48 @@
         w_copy(3, wt.at[at_x(2), w_low], at_x(-1)),
     ]
     loads[0].wait()
-    w_steps[0].start()
-    w_steps[1].start()
+    lead = 1
+    early = s < lead
+
+    def w_begin():
+        w_steps[0].start()
+        w_steps[1].start()
+
+    pl.when(jnp.logical_not(early))(w_begin)
 
     loads[3].wait()
     for g in range(group):
         qh, ql = halves(qv[g] * (hd ** -0.5))
         qcat[g, :, :hd] = qh
         qcat[g, :, hd:] = ql
+    kcat[...] = jnp.zeros_like(kcat)
+    klow[...] = jnp.zeros_like(klow)
+    vcat[...] = jnp.zeros_like(vcat)
     kv_take(s)
-    for n in range(pieces):
-        kv_from(0, n).wait_recv()
-        kv_out(4, n).start()
-        if n < pieces // 2:
-            kv_out(6, n).start()
-        kv_from(1, n).wait_recv()
-        kv_out(5, n).start()
-        if n >= pieces // 2:
-            kv_out(6, n).start()
-    kv_take(at_z(-2))
-    kv_take(at_z(2))
+    def kv_second():
+        for n in range(pieces):
+            kv_from(0, n).wait_recv()
+            kv_out(4, n).start()
+            if n < pieces // 2:
+                kv_out(6, n).start()
+            kv_from(1, n).wait_recv()
+            kv_out(5, n).start()
+            if n >= pieces // 2:
+                kv_out(6, n).start()
+
+    @pl.when(s > 0)
+    def _():
+        kv_second()
+        kv_take(at_z(-2))
+        kv_take(at_z(2))
+
     for i in range(2, len(hops)):
-        for n in range(pieces):
-            kv_from(i, n).wait_recv()
-        kv_take(at_z(-hops[i]))
+        @pl.when(at_z(-hops[i]) < s)
+        def _():
+            for n in range(pieces):
+                kv_from(i, n).wait_recv()
+            kv_take(at_z(-hops[i]))
+
 
     def rs_copy(d, g):
         to = at_x(d)
@@ -208,8 +226,17 @@
 
     lax.fori_loop(0, group, head, 0)
 
+    @pl.when(s == 0)
+    def _():
+        kv_second()
+
+    pl.when(early)(w_begin)
+
     def a_copy(i, g, slot, where):
-        return remote(abuf.at[slot, g], abuf.at[slot, g], a_send.at[i, g], a_recv.at[i, g], {"seq": where})
+        return remote(abuf.at[slot, g], abuf.at[slot, g], a_send.at[i, g], a_recv.at[slot, g], {"seq": where})
+
+    def a_wait(slot, g):
+        a_copy(0, g, slot, right).wait_recv()
 
     ringed = 2
 
@@ -226,29 +253,39 @@
         denominator = jnp.sum(jnp.where(diagonal, line, 0.0), axis=1, keepdims=True)
         abuf[s, g] = total / (denominator + 1.0)
         if g < ringed:
-            a_copy(0, g, s, right).start()
-            a_copy(half, g, s, left).start()
+            @pl.when(early)
+            def _():
+                for i in range(4):
+                    a_out(i, g).start()
+
+            @pl.when(jnp.logical_not(early))
+            def _():
+                r_out(0, g).start()
+                r_out(4, g).start()
+
         else:
             for i in range(4):
                 a_out(i, g).start()
 
-    def a_last(g):
-        if g % 2 == 0:
-            return a_copy(half - 1, g, at_z(1 - half), right)
-        return a_copy(half - 1, g, at_z(half - 1), left)
+    def r_out(i, g):
+        if i == 3:
+            step = 2 if g % 2 == 0 else -2
+            return a_copy(7 + i, g, at_z(-step), at_z(step))
+        if i < 3:
+            return a_copy(7 + i, g, at_z(-i), right)
+        return a_copy(7 + i, g, at_z(i - 4), left)
+
+    def relay_acts(t, g):
+        for slot, i, parity in ((at_z(-t), t, 0), (at_z(t), 4 + t, 1)):
+            yield slot, [i, 3] if t == 2 and g % 2 == parity else [i]
 
     def relay(t, g):
-        a_copy(t - 1, g, at_z(-t), right).wait_recv()
-        if t < half:
-            a_copy(half + t - 1, g, at_z(t), left).wait_recv()
-        if t < half - 1:
-            a_copy(t, g, at_z(-t), right).start()
-            a_copy(half + t, g, at_z(t), left).start()
-        if t == half - 1:
-            a_last(g).start()
-
-    def a_from(i, g):
-        return a_copy(i, g, at_z(-hops[i]), right)
+        for slot, acts in relay_acts(t, g):
+            @pl.when(slot >= lead)
+            def _():
+                a_wait(slot, g)
+                for i in acts:
+                    r_out(i, g).start()
 
     def a_out(i, g):
         if i < 4:
@@ -259,22 +296,39 @@
         step = 2 if g % 2 == 0 else -2
         return a_copy(i, g, at_z(-step), at_z(step))
 
+    def pass_acts(g):
+        for slot, i, parity in ((at_z(-2), 4, 0), (at_z(2), 5, 1)):
+            yield slot, [6, i] if g % 2 == parity else [i]
+
+    def pass_on(g, which):
+        for slot, acts in pass_acts(g):
+            @pl.when(which(slot))
+            def _():
+                a_wait(slot, g)
+                for i in acts:
+                    a_out(i, g).start()
+
+    def first(g):
+        pass_on(g, lambda slot: slot < lead)
+
     def forward(g):
-        a_from(0, g).wait_recv()
-        if g % 2 == 0:
-            a_out(6, g).start()
-        a_out(4, g).start()
-        a_from(1, g).wait_recv()
-        if g % 2 == 1:
-            a_out(6, g).start()
-        a_out(5, g).start()
-
-    def arrived(*distances):
-        for g in range(ringed, group):
-            for distance in distances:
-                for i, hop in enumerate(hops):
-                    if abs(hop) == distance:
-                        a_from(i, g).wait_recv()
+        pass_on(g, lambda slot: slot >= lead)
+
+    def arrived(slots):
+        for slot in slots:
+            away = lax.rem(s - slot + count, count)
+            one = (away == 1) | (away == count - 1)
+            far = (away > 2) & (away < count - 2)
+
+            @pl.when(far | (one & (slot < lead)))
+            def _():
+                for g in range(ringed):
+                    a_wait(slot, g)
+
+            @pl.when(far | one)
+            def _():
+                for g in range(ringed, group):
+                    a_wait(slot, g)
 
     def split_weights(p):
         high, low = halves(wt[p])
@@ -360,14 +414,31 @@
                 c0_copy(i).start()
 
 
-    steps = [[s]] + [[at_z(-1), at_z(1)], [at_z(-2), at_z(2)], [at_z(-3), at_z(3), at_z(4)]]
+    def in_turn(place):
+        chosen = jnp.int32(0)
+        for here in range(count):
+            def away(i):
+                steps = min((here - i) % count, (i - here) % count)
+                return 0.5 if i == 0 and steps > 2 else steps
+
+            chosen = jnp.where(s == here, sorted(range(count), key=away)[place], chosen)
+        return chosen
+
+    steps = [[in_turn(n), in_turn(n + 1)] for n in range(0, count, 2)]
+    first(0)
+    first(1)
+    first(2)
     normalize(0)
+    first(3)
     normalize(1)
+    first(4)
     normalize(2)
+    pl.when(early)(lambda: normalize(3))
+    pl.when(early)(lambda: normalize(4))
     relay(1, 0)
-    normalize(3)
+    pl.when(jnp.logical_not(early))(lambda: normalize(3))
     relay(1, 1)
-    normalize(4)
+    pl.when(jnp.logical_not(early))(lambda: normalize(4))
     w_takes[0].wait_recv()
     w_takes[1].wait_recv()
     w_steps[2].start()
@@ -383,22 +454,20 @@
     w_takes[2].wait_recv()
     w_takes[3].wait_recv()
     split_weights(at_x(2))
+    arrived(steps[0])
     project(steps[0])
-    relay(3, 0)
-    arrived(1)
+    arrived(steps[1])
     project(steps[1])
-    relay(3, 1)
     merge(steps[0])
+    arrived(steps[2])
     project(steps[2])
     merge(steps[1])
+    arrived(steps[3])
+    project(steps[3])
     merge(steps[2])
-    relay(4, 0)
-    relay(4, 1)
-    arrived(3, 4)
-    project(steps[3])
-    merge(steps[3])
     pl.semaphore_wait(cross_known, 1)
     finish(steps[0])
+    merge(steps[3])
     finish(steps[1])
     finish(steps[2])
     finish(steps[3])
@@ -406,6 +475,12 @@
     for i in range(len(hops)):
         for n in range(pieces):
             kv_out(i, n).wait_send()
+    for i in range(2, len(hops)):
+        @pl.when(at_z(-hops[i]) > s)
+        def _():
+            for n in range(pieces):
+                kv_from(i, n).wait_recv()
+
     for copy in w_steps:
         copy.wait_send()
 
@@ -418,10 +493,29 @@
     lax.fori_loop(0, group, drain, 0)
     for g in range(group):
         if g < ringed:
-            for t in range(half - 1):
-                a_copy(t, g, at_z(-t), right).wait_send()
-                a_copy(half + t, g, at_z(t), left).wait_send()
-            a_last(g).wait_send()
+            @pl.when(early)
+            def _():
+                for i in range(4):
+                    a_out(i, g).wait_send()
+
+            @pl.when(jnp.logical_not(early))
+            def _():
+                r_out(0, g).wait_send()
+                r_out(4, g).wait_send()
+
+            for t in (1, 2):
+                for slot, acts in relay_acts(t, g):
+                    @pl.when(slot >= lead)
+                    def _():
+                        for i in acts:
+                            r_out(i, g).wait_send()
+
+            for slot, acts in pass_acts(g):
+                @pl.when(slot < lead)
+                def _():
+                    for i in acts:
+                        a_out(i, g).wait_send()
+
         else:
             for i in range(len(hops)):
                 a_out(i, g).wait_send()
@@ -516,8 +610,8 @@
             dma((parts - 1, group)),
             dma((parts - 1, group)),
             dma((parts - 1, group)),
-            dma((count - 1, group)),
-            dma((count - 1, group)),
+            dma((2 * count - 2, group)),
+            dma((count, group)),
             dma((count,)),
             dma((half,)),
             dma((half, parts - 1)),

time: 58.5 us -> 57.3 us (0.979)
  the two profiles are of different devices: /device:TPU:1 before, /device:TPU:32 now
where the time goes in v5:
time: 57.3 us; the launch traced here: 57.2 us
  Pallas kernels  56.5 us (99%)
  local copies, waits for them, and re-layouts  0.67 us (1%)
    pallas_call x1, Pallas kernels, local(): pl.pallas_call(kernel, out_shape=pltpu.VMEM((quarter, half * wide), F32),...  56.5 us

profile of v5, /device:TPU:32, one launch (start us, length us, event | category | flops | bytes accessed | tf_op | source)
XLA Modules:
  0.0 57.2 jit_solution(15018331224852449618)
XLA Ops:
  0.0 56.5 %power_attention.1 = f32[64,640]{1,0:T(8,128)S(1)} custom-call(f32[5,256,128]{2,1,0:T(8,128)} %bitcast.4, f32[256,128]{1,0:T(8,128)} %bitcast.6, f32[256,128]{1,0:T(8,128)} %bitcast.7, f32[160,640]{1,0:T(8,128)} %bitcast.5), custom_call_target="tpu_custom_call" | custom-call | tf_op jit(solution)/shard_map/power_attention/pallas_call | solution.py:579
  56.5 0.7 %copy.6 = f32[64,640]{1,0:T(8,128)} copy(f32[64,640]{1,0:T(8,128)S(1)} %power_attention.1) | data formatting | bytes 327680

commit v6 on v5

--- a/solution.py
+++ b/solution.py
@@ -238,7 +238,7 @@
     def a_wait(slot, g):
         a_copy(0, g, slot, right).wait_recv()
 
-    ringed = 2
+    ringed = 3
 
     def normalize(g):
         for d in range(1, parts):
@@ -419,7 +419,7 @@
         for here in range(count):
             def away(i):
                 steps = min((here - i) % count, (i - here) % count)
-                return 0.5 if i == 0 and steps > 2 else steps
+                return (0.5, 2.5)[i] if i < 2 and steps > 2 else steps
 
             chosen = jnp.where(s == here, sorted(range(count), key=away)[place], chosen)
         return chosen
@@ -445,32 +445,37 @@
     w_steps[3].start()
     for p in (0, -1, 1):
         split_weights(at_x(p))
+    relay(1, 2)
     relay(2, 0)
-    forward(2)
+    forward(3)
     relay(2, 1)
-    forward(3)
     known()
-    forward(4)
     w_takes[2].wait_recv()
     w_takes[3].wait_recv()
     split_weights(at_x(2))
+    forward(4)
     arrived(steps[0])
     project(steps[0])
+    pl.when(c == 0)(lambda: merge(steps[0]))
+    relay(2, 2)
     arrived(steps[1])
     project(steps[1])
-    merge(steps[0])
+    pl.when(c == 0)(lambda: merge(steps[1]))
     arrived(steps[2])
     project(steps[2])
-    merge(steps[1])
+    pl.when(c == 1)(lambda: merge(steps[0]))
+    pl.when(c == 1)(lambda: merge(steps[1]))
+    pl.when(c == 0)(lambda: merge(steps[2]))
     arrived(steps[3])
     project(steps[3])
-    merge(steps[2])
+    pl.when(c == 0)(lambda: merge(steps[3]))
+    pl.when(c == 1)(lambda: merge(steps[2]))
+    pl.when(c == 1)(lambda: merge(steps[3]))
     pl.semaphore_wait(cross_known, 1)
     finish(steps[0])
-    merge(steps[3])
     finish(steps[1])
+    finish(steps[3])
     finish(steps[2])
-    finish(steps[3])
 
     for i in range(len(hops)):
         for n in range(pieces):

time: 57.3 us -> 55.6 us (0.970)
  the two profiles are of different devices: /device:TPU:32 before, /device:TPU:33 now
where the time goes in v6:
time: 55.6 us; the launch traced here: 55.5 us
  Pallas kernels  54.8 us (99%)
  local copies, waits for them, and re-layouts  0.67 us (1%)
    pallas_call x1, Pallas kernels, local(): pl.pallas_call(kernel, out_shape=pltpu.VMEM((quarter, half * wide), F32),...  54.8 us

profile of v6, /device:TPU:33, one launch (start us, length us, event | category | flops | bytes accessed | tf_op | source)
XLA Modules:
  0.0 55.5 jit_solution(7039543469140054345)
XLA Ops:
  0.0 54.8 %power_attention.1 = f32[64,640]{1,0:T(8,128)S(1)} custom-call(f32[5,256,128]{2,1,0:T(8,128)} %bitcast.4, f32[256,128]{1,0:T(8,128)} %bitcast.6, f32[256,128]{1,0:T(8,128)} %bitcast.7, f32[160,640]{1,0:T(8,128)} %bitcast.5), custom_call_target="tpu_custom_call" | custom-call | tf_op jit(solution)/shard_map/power_attention/pallas_call | solution.py:584
  54.8 0.7 %copy.6 = f32[64,640]{1,0:T(8,128)} copy(f32[64,640]{1,0:T(8,128)S(1)} %power_attention.1) | data formatting | bytes 327680

commit v7 on v6

--- a/solution.py
+++ b/solution.py
@@ -238,7 +238,7 @@
     def a_wait(slot, g):
         a_copy(0, g, slot, right).wait_recv()
 
-    ringed = 3
+    ringed = 4
 
     def normalize(g):
         for d in range(1, parts):
@@ -437,27 +437,28 @@
     pl.when(early)(lambda: normalize(4))
     relay(1, 0)
     pl.when(jnp.logical_not(early))(lambda: normalize(3))
-    relay(1, 1)
-    pl.when(jnp.logical_not(early))(lambda: normalize(4))
     w_takes[0].wait_recv()
     w_takes[1].wait_recv()
     w_steps[2].start()
     w_steps[3].start()
+    relay(1, 1)
+    pl.when(jnp.logical_not(early))(lambda: normalize(4))
     for p in (0, -1, 1):
         split_weights(at_x(p))
     relay(1, 2)
     relay(2, 0)
-    forward(3)
+    relay(1, 3)
     relay(2, 1)
     known()
     w_takes[2].wait_recv()
     w_takes[3].wait_recv()
     split_weights(at_x(2))
     forward(4)
+    relay(2, 2)
     arrived(steps[0])
     project(steps[0])
     pl.when(c == 0)(lambda: merge(steps[0]))
-    relay(2, 2)
+    relay(2, 3)
     arrived(steps[1])
     project(steps[1])
     pl.when(c == 0)(lambda: merge(steps[1]))
@@ -469,8 +470,8 @@
     arrived(steps[3])
     project(steps[3])
     pl.when(c == 0)(lambda: merge(steps[3]))
+    pl.when(c == 1)(lambda: merge(steps[3]))
     pl.when(c == 1)(lambda: merge(steps[2]))
-    pl.when(c == 1)(lambda: merge(steps[3]))
     pl.semaphore_wait(cross_known, 1)
     finish(steps[0])
     finish(steps[1])

time: 55.6 us -> 55.8 us (level)
  no operation moved by 1% of the time
where the time goes in v7:
time: 55.8 us; the launch traced here: 55.7 us
  Pallas kernels  55 us (99%)
  local copies, waits for them, and re-layouts  0.67 us (1%)
    pallas_call x1, Pallas kernels, local(): pl.pallas_call(kernel, out_shape=pltpu.VMEM((quarter, half * wide), F32),...  55 us

profile of v7, /device:TPU:33, one launch (start us, length us, event | category | flops | bytes accessed | tf_op | source)
XLA Modules:
  0.0 55.7 jit_solution(7773674470937491342)
XLA Ops:
  0.0 55.0 %power_attention.1 = f32[64,640]{1,0:T(8,128)S(1)} custom-call(f32[5,256,128]{2,1,0:T(8,128)} %bitcast.4, f32[256,128]{1,0:T(8,128)} %bitcast.6, f32[256,128]{1,0:T(8,128)} %bitcast.7, f32[160,640]{1,0:T(8,128)} %bitcast.5), custom_call_target="tpu_custom_call" | custom-call | tf_op jit(solution)/shard_map/power_attention/pallas_call | solution.py:585
  55.0 0.7 %copy.6 = f32[64,640]{1,0:T(8,128)} copy(f32[64,640]{1,0:T(8,128)S(1)} %power_attention.1) | data formatting | bytes 327680

commit v8 on v6

--- a/solution.py
+++ b/solution.py
@@ -219,7 +219,7 @@
             rs_src[g, p] = numerator[part]
             spread = jnp.where(diagonal, jnp.broadcast_to(denominator[part], (quarter, hd)), 0.0)
             den_src[g, p] = jnp.sum(spread, axis=0, keepdims=True)
-        for d in range(1, parts):
+        for d in (2, 1, 3):
             den_copy(d, g).start()
             rs_copy(d, g).start()
         return carry
@@ -365,7 +365,7 @@
                 c0_copy(i).wait_recv()
                 for p in range(parts):
                     cpk[i, p] = cpk[i, p] + c0r[lax.rem(i, half), p]
-                for d in range(1, parts):
+                for d in (2, 1, 3):
                     c1_copy(i, d).start()
 
     def finish(slots):

time: 55.6 us -> 55.5 us (level)
  no operation moved by 1% of the time
where the time goes in v8:
time: 55.5 us; the launch traced here: 55.4 us
  Pallas kernels  54.7 us (99%)
  local copies, waits for them, and re-layouts  0.67 us (1%)
    pallas_call x1, Pallas kernels, local(): pl.pallas_call(kernel, out_shape=pltpu.VMEM((quarter, half * wide), F32),...  54.7 us

profile of v8, /device:TPU:33, one launch (start us, length us, event | category | flops | bytes accessed | tf_op | source)
XLA Modules:
  0.0 55.4 jit_solution(14893659471468898233)
XLA Ops:
  0.0 54.7 %power_attention.1 = f32[64,640]{1,0:T(8,128)S(1)} custom-call(f32[5,256,128]{2,1,0:T(8,128)} %bitcast.4, f32[256,128]{1,0:T(8,128)} %bitcast.6, f32[256,128]{1,0:T(8,128)} %bitcast.7, f32[160,640]{1,0:T(8,128)} %bitcast.5), custom_call_target="tpu_custom_call" | custom-call | tf_op jit(solution)/shard_map/power_attention/pallas_call | solution.py:584
  54.7 0.7 %copy.6 = f32[64,640]{1,0:T(8,128)} copy(f32[64,640]{1,0:T(8,128)S(1)} %power_attention.1) | data formatting | bytes 327680
